TPU v7x, 256 devices: a whole 4x4x8 slice. The times are simulated.
256 devices in a mesh: shard: 8 (over z_lo, x), tensor: 4 (over z_hi), section: 8 (over y, core).
Axes of the slice: x: 4, y: 4, z: 8 (z_hi: 4, z_lo: 2; z = z_hi * 2 + z_lo), core: 2. Of those that a mesh axis runs over, the one named last changes fastest.
Arguments:
- activations: bfloat16 [8, 2048, 2304], P(None, 'shard', ('tensor', 'section')), may hold values from -6 to 6
- router_grad: bfloat16 [8, 2048], P(None, 'shard'), may hold values from -6 to 6
- token_ids: int32 [2048], P('shard'), may hold values from 0 to 8191
- norm_terms: bfloat16 [2, 2048, 2304], P(None, 'shard', ('tensor', 'section'))
- old_factors: float32 [8, 2304, 2304], P('shard', 'tensor', 'section'), as said below
- old_router_factor: float32 [8, 8], replicated, as said below
- old_norm_diag: float32 [2, 2304], P(None, ('tensor', 'section')), may hold values from 0.5 to 5
- old_embed_diag: float32 [8192], P('tensor'), may hold values from 0.05 to 0.5
Outputs:
- precond_attn: float32 [4, 2304, 2304], P(None, 'tensor', 'section')
- precond_router: float32 [8, 2304], P(None, 'tensor')
- precond_norms: float32 [2, 2304], P(None, ('tensor', 'section'))
- precond_embed: float32 [8192, 2304], P('tensor', 'section')
Inputs may be any that keep to these rules, and one draw needn't show every extreme that they name: `old_factors`: each matrix is symmetric with a positive diagonal. `old_router_factor`: symmetric with a positive diagonal.
All inputs are finite; a program needn't handle non-finite values.
Results may differ from a plain program's by a relative error of at most 0.0083.
Values may be sent and summed in bfloat16 or wider, within the bound.
A program may use at most 64 MiB of HBM per device.

v0:
```python
import math
import jax
import jax.numpy as jnp
from jax import lax
from jax.sharding import PartitionSpec as P

D = 2304
EXPERTS = 8
VOCAB = 8192
factor_decay = 0.5
damping = 0.01
learning_rate = 0.05


def local_inverse(matrix):
    width = matrix.shape[0]
    trace = jnp.sum(jnp.diagonal(matrix))
    factor_scale = width / (3.0 * trace)
    identity = jnp.eye(width, dtype=jnp.float32)
    matrix_low = lax.optimization_barrier(matrix.astype(jnp.bfloat16))
    first = 2.0 * factor_scale * identity - factor_scale * factor_scale * matrix_low.astype(
        jnp.float32
    )
    first_low = first.astype(jnp.bfloat16)
    image = jnp.dot(matrix_low, first_low, preferred_element_type=jnp.float32).astype(jnp.bfloat16)
    product = jnp.dot(first_low, image, preferred_element_type=jnp.float32)
    return (2.0 * first - product).astype(jnp.bfloat16)


def fold_with(columns, piece):
    return jnp.einsum("kij,kjl->kil", piece, columns, preferred_element_type=jnp.float32)


def per_device(
    activations,
    router_grad,
    token_ids,
    norm_terms,
    old_factors,
    old_router_factor,
    old_norm_diag,
    old_embed_diag,
):
    n_tensor = lax.axis_size("tensor")
    n_section = lax.axis_size("section")
    n_shard = lax.axis_size("shard")
    tensor_rank = lax.axis_index("tensor")
    section_rank = lax.axis_index("section")
    row_block = D // n_tensor
    col_block = D // n_section
    tokens_all = activations.shape[1] * n_shard
    row_start = tensor_rank * row_block
    col_start = section_rank * col_block

    def collect(carry, piece):
        whole = lax.all_gather(piece, ("tensor", "section"), axis=1, tiled=True)
        rows_part = lax.dynamic_slice_in_dim(whole, row_start, row_block, 1)
        cols_part = lax.dynamic_slice_in_dim(whole, col_start, col_block, 1)
        return (carry, (rows_part, cols_part))

    unused_carry, (row_parts, col_parts) = lax.scan(collect, jnp.int32(0), activations)
    partial_value = jnp.einsum(
        "mnr,mnc->mrc", row_parts, col_parts, preferred_element_type=jnp.float32
    )
    fresh = lax.psum_scatter(partial_value, "shard", scatter_dimension=0, tiled=True) / tokens_all
    row_index = lax.broadcasted_iota(jnp.int32, (row_block, col_block), 0) + row_start
    col_index = lax.broadcasted_iota(jnp.int32, (row_block, col_block), 1) + col_start
    eye_block = (row_index == col_index).astype(jnp.float32)
    matrix = factor_decay * old_factors + (1.0 - factor_decay) * fresh + damping * eye_block
    diag_part = jnp.sum(matrix * eye_block, axis=(1, 2))
    trace = lax.psum(diag_part, ("tensor", "section"))
    factor_scale = (D / (3.0 * trace))[:, None, None]
    matrix_low = lax.optimization_barrier(matrix.astype(jnp.bfloat16))
    first = 2.0 * factor_scale * eye_block - factor_scale * factor_scale * matrix_low.astype(
        jnp.float32
    )
    first_low = first.astype(jnp.bfloat16)
    first_cols = lax.all_gather(first_low, "tensor", axis=1, tiled=True)
    image = fold_with(first_cols, lax.all_gather(matrix_low, "section", axis=2, tiled=True))
    image_cols = lax.all_gather(image.astype(jnp.bfloat16), "tensor", axis=1, tiled=True)
    product = fold_with(image_cols, lax.all_gather(first_low, "section", axis=2, tiled=True))
    inverse_low = (2.0 * first - product).astype(jnp.bfloat16)
    inverses = lax.all_gather(inverse_low, "shard", axis=0, tiled=True)
    left_terms = jnp.stack(
        [
            jnp.einsum("nc,rc->nr", col_parts[m], inverses[m], preferred_element_type=jnp.float32)
            for m in (0, 4, 6)
        ]
    )
    left = lax.psum(left_terms, "section").astype(jnp.bfloat16)
    right_terms = jnp.stack(
        [
            jnp.einsum("nr,rc->nc", row_parts[m], inverses[m], preferred_element_type=jnp.float32)
            for m in (1, 2, 3, 5, 7)
        ]
    )
    right = lax.psum(right_terms, "tensor").astype(jnp.bfloat16)
    norm_values = norm_terms.astype(jnp.float32)
    router_part = jnp.einsum(
        "en,fn->ef", router_grad, router_grad, preferred_element_type=jnp.float32
    )
    router_sum, norm_total, norm_squares = lax.psum(
        (router_part, jnp.sum(norm_values, axis=1), jnp.sum(norm_values * norm_values, axis=1)),
        "shard",
    )
    router_matrix = (
        factor_decay * old_router_factor
        + (1.0 - factor_decay) * (router_sum / tokens_all)
        + damping * jnp.eye(EXPERTS, dtype=jnp.float32)
    )
    router_inverse = local_inverse(router_matrix)
    router_right = jnp.einsum(
        "en,ef->nf", router_grad, router_inverse, preferred_element_type=jnp.float32
    ).astype(jnp.bfloat16)
    precond_norms = (
        learning_rate
        * norm_total
        / (
            factor_decay * old_norm_diag
            + (1.0 - factor_decay) * (norm_squares / tokens_all)
            + damping
        )
    )
    ids_all = lax.all_gather(token_ids, "shard", axis=0, tiled=True)
    embed_all = lax.all_gather(right[4], "shard", axis=0, tiled=True)
    paired_left = jnp.stack([left[0], left[0], left[0], left[1]])
    attn_terms = jnp.einsum(
        "wnr,wnc->wrc", paired_left, right[:4], preferred_element_type=jnp.float32
    )
    router_term = jnp.einsum("nf,nr->fr", router_right, left[2], preferred_element_type=jnp.float32)
    attn_sum, router_total = lax.psum((attn_terms, router_term), "shard")
    precond_attn = learning_rate * attn_sum
    precond_router = learning_rate * router_total
    vocab_block = VOCAB // n_tensor
    step_rows = math.gcd(vocab_block, 512)
    vocab_start = tensor_rank * vocab_block

    def embed_block(block_index):
        ids_here = vocab_start + block_index * step_rows + lax.iota(jnp.int32, step_rows)
        onehot = (ids_here[:, None] == ids_all[None, :]).astype(jnp.bfloat16)
        summed = jnp.dot(onehot, embed_all, preferred_element_type=jnp.float32)
        tallies = jnp.sum(onehot, axis=1, dtype=jnp.float32)
        return (summed, tallies)

    block_sums, block_counts = lax.map(
        embed_block, jnp.arange(vocab_block // step_rows, dtype=jnp.int32)
    )
    embed_sum = block_sums.reshape(vocab_block, col_block)
    counts = block_counts.reshape(vocab_block)
    divisor = factor_decay * old_embed_diag + (1.0 - factor_decay) * (counts / tokens_all) + damping
    precond_embed = learning_rate * embed_sum / divisor[:, None]
    return (precond_attn, precond_router, precond_norms, precond_embed)


def solution(mesh):
    return jax.shard_map(
        per_device,
        mesh=mesh,
        in_specs=(
            P(None, "shard", ("tensor", "section")),
            P(None, "shard"),
            P("shard"),
            P(None, "shard", ("tensor", "section")),
            P("shard", "tensor", "section"),
            P(),
            P(None, ("tensor", "section")),
            P("tensor"),
        ),
        out_specs=(
            P(None, "tensor", "section"),
            P(None, "tensor"),
            P(None, ("tensor", "section")),
            P("tensor", "section"),
        ),
        check_vma=False,
    )
```

profile of v0, /device:TPU:8, one launch (start us, length us, event | category | flops | bytes accessed | tf_op | source)
XLA Modules:
  0.0 1097.6 jit_solution(1544421095464947552)
XLA Ops:
  8.0 450.4 %while.26 = (s32[]{:T(128)}, bf16[8,256,576]{1,2,0:T(8,128)(2,1)S(1)}, bf16[8,256,288]{1,2,0:T(8,128)(2,1)S(1)}, bf16[8,256,72]{1,2,0:T(8,128)(2,1)}, s32[]{:T(128)}, /*index=5*/s32[]{:T(128)}, s32[]{:T(128)}) while((s32[]{:T(128)}, bf16[8,256,576]{1,2,0:T(8,128)(2,1)S(1)}, bf16[8,256,288]{1,2,0:T(8,128)(2,1)S(1)}, ...), condition=%wide.region_1.2_spmd, body=%wide.region_0.1_spmd.sunk | while | flops 2 | bytes 4608145 | solution.py:61
  8.1 1.4 constant_dynamic-slice_fusion.2
  9.5 56.6 %all-gather.27.cloned.1.call-done = bf16[1,256,2304]{1,2,0:T(8,128)(2,1)} async-done(((bf16[1,256,72]{1,2,0:T(8,128)(2,1)}), bf16[1,256,2304]{1,2,0:T(8,128)(2,1)}) %all-gather.27.cloned.1.call-update) | async-done | bytes 1179664 | tf_op jit(solution)/shard_map/while/body/eval_jaxpr/all_gather | solution.py:56
  69.5 52.5 %all-gather.27.cloned.1.call-done = bf16[1,256,2304]{1,2,0:T(8,128)(2,1)} async-done(((bf16[1,256,72]{1,2,0:T(8,128)(2,1)}), bf16[1,256,2304]{1,2,0:T(8,128)(2,1)}) %all-gather.27.cloned.1.call-update) | async-done | bytes 1179664 | tf_op jit(solution)/shard_map/while/body/eval_jaxpr/all_gather | solution.py:56
  125.4 52.5 %all-gather.27.cloned.1.call-done = bf16[1,256,2304]{1,2,0:T(8,128)(2,1)} async-done(((bf16[1,256,72]{1,2,0:T(8,128)(2,1)}), bf16[1,256,2304]{1,2,0:T(8,128)(2,1)}) %all-gather.27.cloned.1.call-update) | async-done | bytes 1179664 | tf_op jit(solution)/shard_map/while/body/eval_jaxpr/all_gather | solution.py:56
  181.3 52.2 %all-gather.27.cloned.1.call-done = bf16[1,256,2304]{1,2,0:T(8,128)(2,1)} async-done(((bf16[1,256,72]{1,2,0:T(8,128)(2,1)}), bf16[1,256,2304]{1,2,0:T(8,128)(2,1)}) %all-gather.27.cloned.1.call-update) | async-done | bytes 1179664 | tf_op jit(solution)/shard_map/while/body/eval_jaxpr/all_gather | solution.py:56
  236.9 52.2 %all-gather.27.cloned.1.call-done = bf16[1,256,2304]{1,2,0:T(8,128)(2,1)} async-done(((bf16[1,256,72]{1,2,0:T(8,128)(2,1)}), bf16[1,256,2304]{1,2,0:T(8,128)(2,1)}) %all-gather.27.cloned.1.call-update) | async-done | bytes 1179664 | tf_op jit(solution)/shard_map/while/body/eval_jaxpr/all_gather | solution.py:56
  292.5 52.2 %all-gather.27.cloned.1.call-done = bf16[1,256,2304]{1,2,0:T(8,128)(2,1)} async-done(((bf16[1,256,72]{1,2,0:T(8,128)(2,1)}), bf16[1,256,2304]{1,2,0:T(8,128)(2,1)}) %all-gather.27.cloned.1.call-update) | async-done | bytes 1179664 | tf_op jit(solution)/shard_map/while/body/eval_jaxpr/all_gather | solution.py:56
  348.1 52.5 %all-gather.27.cloned.1.call-done = bf16[1,256,2304]{1,2,0:T(8,128)(2,1)} async-done(((bf16[1,256,72]{1,2,0:T(8,128)(2,1)}), bf16[1,256,2304]{1,2,0:T(8,128)(2,1)}) %all-gather.27.cloned.1.call-update) | async-done | bytes 1179664 | tf_op jit(solution)/shard_map/while/body/eval_jaxpr/all_gather | solution.py:56
  404.0 52.5 %all-gather.27.cloned.1.call-done = bf16[1,256,2304]{1,2,0:T(8,128)(2,1)} async-done(((bf16[1,256,72]{1,2,0:T(8,128)(2,1)}), bf16[1,256,2304]{1,2,0:T(8,128)(2,1)}) %all-gather.27.cloned.1.call-update) | async-done | bytes 1179664 | tf_op jit(solution)/shard_map/while/body/eval_jaxpr/all_gather | solution.py:56
  458.5 3.7 fusion.83
  462.3 70.5 %reduce-scatter.2.cloned.1.call-done = f32[1,576,288]{1,2,0:T(8,128)} async-done(((f32[8,576,288]{1,2,0:T(8,128)}), f32[1,576,288]{1,2,0:T(8,128)}) %reduce-scatter.2.cloned.1.call-update) | async-done | bytes 663568 | tf_op jit(solution)/shard_map/reduce_scatter | solution.py:65
  532.8 2.1 fusion.48
  534.9 69.3 %psum.56 = f32[1]{0:T(128)} all-reduce(f32[1]{0:T(128)} %bitcast.4), channel_id=1, replica_groups=mesh['shard'=8,'tensor'=4,'section'=8] {'tensor','section'}, use_global_device_ids=true, to_apply=%region_4.5 | all-reduce | flops 1 | bytes 8 | tf_op jit(solution)/shard_map/psum | solution.py:71
  605.1 1.9 copy.32
  607.7 65.6 %all-gather.19.cloned.1.call-done = bf16[1,2304,288]{2,0,1:T(2,128)(2,1)} async-done(((bf16[1,576,288]{2,0,1:T(2,128)(2,1)}), bf16[1,2304,288]{2,0,1:T(2,128)(2,1)}) %all-gather.19.cloned.1.call-update) | async-done | bytes 1327120 | tf_op jit(solution)/shard_map/all_gather | solution.py:78
  673.3 8.4 copy.33
  681.7 29.2 %all-gather.17.cloned.1.call-done = bf16[1,576,2304]{1,2,0:T(8,128)(2,1)} async-done(((bf16[1,576,288]{1,2,0:T(8,128)(2,1)}), bf16[1,576,2304]{1,2,0:T(8,128)(2,1)}) %all-gather.17.cloned.1.call-update) | async-done | bytes 2654224 | tf_op jit(solution)/shard_map/all_gather | solution.py:79
  710.9 3.8 fusion.29
  715.5 41.7 %all-gather.25.cloned.1.call-done = bf16[4,576,288]{1,2,0:T(8,128)(2,1)} async-done(((bf16[1,576,288]{1,2,0:T(8,128)(2,1)}), bf16[4,576,288]{1,2,0:T(8,128)(2,1)}) %all-gather.25.cloned.1.call-update) | async-done | bytes 1327120 | tf_op jit(solution)/shard_map/all_gather | solution.py:80
  757.3 2.1 copy.34
  759.4 2.0 reshape.184
  761.4 24.7 %all-gather.15.cloned.1.call-done = bf16[1,576,2304]{1,2,0:T(8,128)(2,1)} async-done(((bf16[1,576,288]{1,2,0:T(8,128)(2,1)}), bf16[1,576,2304]{1,2,0:T(8,128)(2,1)}) %all-gather.15.cloned.1.call-update) | async-done | bytes 2654224 | tf_op jit(solution)/shard_map/all_gather | solution.py:81
  786.2 4.2 fusion.21
  790.6 19.7 %psum.60 = f32[8,8]{1,0:T(8,128)S(1)} all-reduce(f32[8,8]{1,0:T(8,128)S(1)} %fusion.84), channel_id=1, replica_groups=mesh['shard'=8,'tensor'=4,'section'=8] {'shard'}, use_global_device_ids=true, to_apply=%region_8.9 | all-reduce | flops 64 | bytes 512 | tf_op jit(solution)/shard_map/psum | solution.py:102
  812.3 15.1 %all-gather.4 = s32[8,1,256]{2,1,0:T(1,128)S(1)} all-gather(s32[1,1,256]{2,1,0:T(1,128)S(1)} %bitcast.152), channel_id=1, replica_groups=mesh['shard'=8,'tensor'=4,'section'=8] {'shard'}, dimensions={0}, use_global_device_ids=true | all-gather | bytes 9216 | tf_op jit(solution)/shard_map/all_gather | solution.py:124
  827.8 9.9 all-gather.21.cloned.1.call-done
  837.7 2.0 fusion.44
  839.7 2.0 fusion.43
  841.7 2.0 fusion.42
  843.7 2.0 fusion.41
  845.6 2.0 fusion.40
  847.6 56.9 %all-reduce.6 = bf16[5,256,288]{1,2,0:T(8,128)(2,1)S(1)} all-reduce(f32[5,256,288]{1,2,0:T(8,128)} %fusion.40), channel_id=1, replica_groups=mesh['shard'=8,'tensor'=4,'section'=8] {'tensor'}, use_global_device_ids=true, to_apply=%region_6.7 | all-reduce | flops 368640 | bytes 2211840 | tf_op jit(solution)/shard_map/psum | solution.py:97
  905.2 1.4 convolution_bitcast_fusion.2
  906.7 1.4 convolution_bitcast_fusion.1
  908.1 1.4 convolution_bitcast_fusion
  909.7 48.6 %all-reduce.7 = bf16[3,256,576]{1,2,0:T(8,128)(2,1)S(1)} all-reduce(f32[3,256,576]{1,2,0:T(8,128)S(1)} %pad_maximum_fusion), channel_id=1, replica_groups=mesh['shard'=8,'tensor'=4,'section'=8] {'section'}, use_global_device_ids=true, to_apply=%region_5.6 | all-reduce | flops 442368 | bytes 2654208 | tf_op jit(solution)/shard_map/psum | solution.py:90
  958.6 33.9 %all-reduce = (f32[8,576]{1,0:T(8,128)S(1)}, f32[2,72]{1,0:T(2,128)S(1)}, f32[2,72]{1,0:T(2,128)S(1)}) all-reduce(f32[8,576]{1,0:T(8,128)S(1)} %fusion.45, f32[2,72]{1,0:T(2,128)S(1)} %get-tuple-element.173, f32[2,72]{1,0:T(2,128)S(1)} %get-tuple-element.172), channel_id=1, replica_groups=mesh['shard'=8,'tensor'=4,'section'=8] {'shard'}, use_global_device_ids=true, to_apply=%region_10.11 | all-reduce | flops 4896 | bytes 39168 | tf_op jit(solution)/shard_map/psum | solution.py:131
  993.1 2.3 fusion.34
  996.6 2.5 copy.35
  999.2 17.1 %while.27 = (s32[]{:T(128)}, f32[4,512,288]{1,2,0:T(8,128)S(1)}, f32[4,512]{1,0:T(4,128)S(1)}, s32[4]{0:T(128)S(1)}, s32[]{:T(128)}, /*index=5*/s32[2048]{0:T(10...) while((s32[]{:T(128)}, f32[4,512,288]{1,2,0:T(8,128)S(1)}, f32[4,512]{1,0:T(4,128)S(1)}, ...), condition=%wide.region_17.18_spmd, body=%wide.region_15.17_spmd.sunk | while | flops 609222656 | bytes 1798293 | solution.py:145
  1000.3 2.5 fusion.99
  1004.5 2.5 fusion.99
  1008.8 2.5 fusion.99
  1013.1 2.5 fusion.99
  1017.2 1.7 broadcast_divide_fusion
  1018.9 67.6 %all-reduce.5.cloned.1.call-done = f32[4,576,288]{1,2,0:T(8,128)} async-done(((f32[4,576,288]{1,2,0:T(8,128)}), f32[4,576,288]{1,2,0:T(8,128)}) %all-reduce.5.cloned.1.call-update) | async-done | bytes 2654224 | tf_op jit(solution)/shard_map/psum | solution.py:131
  1086.5 3.7 broadcast_multiply_fusion
  (127 shorter events, 37.7 us)
Async XLA Ops:
  8.0 782.5 %copy-start = (bf16[8,256]{1,0:T(8,128)(2,1)S(1)}, bf16[8,256]{1,0:T(8,128)(2,1)}, u32[]{:S(2)}) copy-start(bf16[8,256]{1,0:T(8,128)(2,1)} %param.13) | copy-start | bytes 12292
  8.1 58.1 %all-gather.27.cloned.1.call-start = ((), (), s32[]{:S(2)}) async-start(), calls=%async_computation.9 | async-start | bytes 1216512 | tf_op jit(solution)/shard_map/while/body/eval_jaxpr/all_gather | solution.py:56
  68.0 54.0 %all-gather.27.cloned.1.call-start = ((), (), s32[]{:S(2)}) async-start(), calls=%async_computation.9 | async-start | bytes 1216512 | tf_op jit(solution)/shard_map/while/body/eval_jaxpr/all_gather | solution.py:56
  124.0 54.0 %all-gather.27.cloned.1.call-start = ((), (), s32[]{:S(2)}) async-start(), calls=%async_computation.9 | async-start | bytes 1216512 | tf_op jit(solution)/shard_map/while/body/eval_jaxpr/all_gather | solution.py:56
  179.9 53.7 %all-gather.27.cloned.1.call-start = ((), (), s32[]{:S(2)}) async-start(), calls=%async_computation.9 | async-start | bytes 1216512 | tf_op jit(solution)/shard_map/while/body/eval_jaxpr/all_gather | solution.py:56
  235.4 53.7 %all-gather.27.cloned.1.call-start = ((), (), s32[]{:S(2)}) async-start(), calls=%async_computation.9 | async-start | bytes 1216512 | tf_op jit(solution)/shard_map/while/body/eval_jaxpr/all_gather | solution.py:56
  291.0 53.7 %all-gather.27.cloned.1.call-start = ((), (), s32[]{:S(2)}) async-start(), calls=%async_computation.9 | async-start | bytes 1216512 | tf_op jit(solution)/shard_map/while/body/eval_jaxpr/all_gather | solution.py:56
  346.6 54.0 %all-gather.27.cloned.1.call-start = ((), (), s32[]{:S(2)}) async-start(), calls=%async_computation.9 | async-start | bytes 1216512 | tf_op jit(solution)/shard_map/while/body/eval_jaxpr/all_gather | solution.py:56
  402.5 54.0 %all-gather.27.cloned.1.call-start = ((), (), s32[]{:S(2)}) async-start(), calls=%async_computation.9 | async-start | bytes 1216512 | tf_op jit(solution)/shard_map/while/body/eval_jaxpr/all_gather | solution.py:56
  458.4 3.7 copy-start.5
  458.5 3.7 copy-start.7
  458.5 74.3 %reduce-scatter.2.cloned.1.call-start = ((), (), s32[]{:S(2)}) async-start(), calls=%async_computation.1 | async-start | bytes 6635520 | tf_op jit(solution)/shard_map/reduce_scatter | solution.py:65
  462.2 70.6 %copy-start.8 = (f32[1,576,288]{1,2,0:T(8,128)S(1)}, f32[1,576,288]{1,2,0:T(8,128)}, u32[]{:S(2)}) copy-start(f32[1,576,288]{1,2,0:T(8,128)} %param.16) | copy-start | bytes 1990660
  462.2 211.0 %all-gather.19.cloned.1.call-start = ((), (), s32[]{:S(2)}) async-start(), calls=%async_computation.4 | async-start | bytes 4423680 | tf_op jit(solution)/shard_map/all_gather | solution.py:78
  534.9 72.2 %copy-start.1 = (bf16[1,576,288]{1,2,0:T(8,128)(2,1)}, bf16[1,576,288]{1,2,0:T(8,128)(2,1)S(1)}, u32[]{:S(2)}) copy-start(bf16[1,576,288]{1,2,0:T(8,128)(2,1)S(1)} %get-tuple-element.206) | copy-start | bytes 995332
  605.1 76.6 %copy-start.3 = (bf16[1,576,288]{1,2,0:T(8,128)(2,1)}, bf16[1,576,288]{1,2,0:T(8,128)(2,1)S(1)}, u32[]{:S(2)}) copy-start(bf16[1,576,288]{1,2,0:T(8,128)(2,1)S(1)} %fusion.50) | copy-start | bytes 995332
  607.1 103.9 %all-gather.17.cloned.1.call-start = ((), (), s32[]{:S(2)}) async-start(), calls=%async_computation.3 | async-start | bytes 3317760 | tf_op jit(solution)/shard_map/all_gather | solution.py:79
  607.6 149.7 %all-gather.25.cloned.1.call-start = ((), (), s32[]{:S(2)}) async-start(), calls=%async_computation.8 | async-start | bytes 1843200 | tf_op jit(solution)/shard_map/all_gather | solution.py:80
  714.7 71.4 %all-gather.15.cloned.1.call-start = ((), (), s32[]{:S(2)}) async-start(), calls=%async_computation.2 | async-start | bytes 3317760 | tf_op jit(solution)/shard_map/all_gather | solution.py:81
  715.5 70.7 %copy-start.2 = (bf16[1,576,288]{1,2,0:T(8,128)(2,1)S(1)}, bf16[1,576,288]{1,2,0:T(8,128)(2,1)}, u32[]{:S(2)}) copy-start(bf16[1,576,288]{1,2,0:T(8,128)(2,1)} %copy-done.1) | copy-start | bytes 995332
  715.5 122.2 %all-gather.21.cloned.1.call-start = ((), (), s32[]{:S(2)}) async-start(), calls=%async_computation.5 | async-start | bytes 3317760 | tf_op jit(solution)/shard_map/all_gather | solution.py:83
  761.4 48.9 %copy-start.11 = (f32[8,8]{1,0:T(8,128)S(1)}, f32[8,8]{1,0:T(8,128)}, u32[]{:S(2)}) copy-start(f32[8,8]{1,0:T(8,128)} %param.17) | copy-start | bytes 772
  761.4 50.8 %copy-start.12 = (s32[256]{0:T(256)S(1)}, s32[256]{0:T(256)}, u32[]{:S(2)}) copy-start(s32[256]{0:T(256)} %param.14) | copy-start | bytes 3076
  761.4 65.9 %copy-start.9 = (bf16[2,256,72]{1,2,0:T(8,128)(2,1)S(1)}, bf16[2,256,72]{1,2,0:T(8,128)(2,1)}, u32[]{:S(2)}) copy-start(bf16[2,256,72]{1,2,0:T(8,128)(2,1)} %param.15) | copy-start | bytes 221188
  761.4 76.3 %copy-start.6 = (bf16[8,256,576]{1,2,0:T(8,128)(2,1)S(1)}, bf16[8,256,576]{1,2,0:T(8,128)(2,1)}, u32[]{:S(2)}) copy-start(bf16[8,256,576]{1,2,0:T(8,128)(2,1)} %copy-done.5) | copy-start | bytes 7077892
  790.4 206.2 %all-gather.23.cloned.1.call-start = ((), (), s32[]{:S(2)}) async-start(), calls=%async_computation.7 | async-start | bytes 1327104 | tf_op jit(solution)/shard_map/all_gather | solution.py:125
  905.2 181.3 %all-reduce.5.cloned.1.call-start = ((), (), s32[]{:S(2)}) async-start(), calls=%async_computation.6 | async-start | bytes 5898240 | tf_op jit(solution)/shard_map/psum | solution.py:131
  995.4 0.7 copy-start.13
  995.4 3.8 copy-start.4
  1016.5 0.7 copy-start.10
Sparse Core Ops, SparseCore 0:
  12.1 53.9 all-gather.26
  72.1 49.8 all-gather.26
  128.0 49.8 all-gather.26
  183.6 49.8 all-gather.26
  239.2 49.8 all-gather.26
  294.8 49.8 all-gather.26
  350.7 49.8 all-gather.26
  406.6 49.8 all-gather.26
Sparse Core Ops, SparseCore 1:
  462.3 70.4 reduce-scatter.1
  607.1 66.1 all-gather.18
  675.1 35.8 all-gather.16
  714.8 42.4 all-gather.24
  759.3 26.8 all-gather.14
  790.5 47.2 all-gather.20
  905.3 39.6 all-gather.22
  995.5 90.9 all-reduce.4
where the time goes:
time: 1100 us
  waiting for transfers between devices  734 us (67%)
  blocking collectives  243 us (22%)
  local copies, waits for them, and re-layouts  48.5 us (4%)
  matrix products  38.8 us (4%)
  between operations  17.2 us (2%)
  other arithmetic  12.2 us (1%)
    all_gather x8, waiting for transfers between devices, collect(): whole = lax.all_gather(piece, ('tensor', 'section'), axis=1, tiled=True)  423 us
    reduce_scatter x1, waiting for transfers between devices, per_device(): lax.psum_scatter(partial_value, 'shard', scatter_dimension=0, tiled=True)  70.5 us
    psum x1, blocking collectives, per_device(): trace = lax.psum(diag_part, ('tensor', 'section'))  69.3 us
    psum x1, waiting for transfers between devices, per_device(): attn_sum, router_total = lax.psum((attn_terms, router_term), 'shard')  67.6 us
    all_gather x1, waiting for transfers between devices, per_device(): first_cols = lax.all_gather(first_low, 'tensor', axis=1, tiled=True)  65.6 us
    psum x1, blocking collectives, per_device(): right = lax.psum(right_terms, 'tensor').astype(jnp.bfloat16)  56.9 us
    psum x1, blocking collectives, per_device(): left = lax.psum(left_terms, 'section').astype(jnp.bfloat16)  48.6 us
    all_gather x1, waiting for transfers between devices, per_device(): lax.all_gather(image.astype(jnp.bfloat16), 'tensor', axis=1, tiled=True)  41.7 us
  transfers between devices with their start and end apart: 16, of which 15 were waited for; matrix products, arithmetic and copies ran while one was open for 4% of the time, Pallas kernels for 0%

commit v1 on v0

--- a/solution.py
+++ b/solution.py
@@ -68,7 +68,7 @@
     eye_block = (row_index == col_index).astype(jnp.float32)
     matrix = factor_decay * old_factors + (1.0 - factor_decay) * fresh + damping * eye_block
     diag_part = jnp.sum(matrix * eye_block, axis=(1, 2))
-    trace = lax.psum(diag_part, ("tensor", "section"))
+    trace = lax.psum(lax.psum(diag_part, "section"), "tensor")
     factor_scale = (D / (3.0 * trace))[:, None, None]
     matrix_low = lax.optimization_barrier(matrix.astype(jnp.bfloat16))
     first = 2.0 * factor_scale * eye_block - factor_scale * factor_scale * matrix_low.astype(

time: 1100 us -> 1050 us (0.955)
  blocking collectives: 243 us -> 199 us
    psum x1 -> x2, blocking collectives: 69.3 us -> 24.7 us  [per_device(): trace = lax.psum(lax.psum(diag_part, 'section'), 'tensor')]
where the time goes in v1:
time: 1050 us
  waiting for transfers between devices  729 us (69%)
  blocking collectives  199 us (19%)
  local copies, waits for them, and re-layouts  49 us (5%)
  matrix products  38.8 us (4%)
  between operations  17.2 us (2%)
  other arithmetic  12.2 us (1%)
    all_gather x8, waiting for transfers between devices, collect(): whole = lax.all_gather(piece, ('tensor', 'section'), axis=1, tiled=True)  423 us
    reduce_scatter x1, waiting for transfers between devices, per_device(): lax.psum_scatter(partial_value, 'shard', scatter_dimension=0, tiled=True)  70.5 us
    psum x1, waiting for transfers between devices, per_device(): attn_sum, router_total = lax.psum((attn_terms, router_term), 'shard')  65.8 us
    all_gather x1, waiting for transfers between devices, per_device(): first_cols = lax.all_gather(first_low, 'tensor', axis=1, tiled=True)  62.8 us
    psum x1, blocking collectives, per_device(): right = lax.psum(right_terms, 'tensor').astype(jnp.bfloat16)  56.8 us
    psum x1, blocking collectives, per_device(): left = lax.psum(left_terms, 'section').astype(jnp.bfloat16)  48.2 us
    all_gather x1, waiting for transfers between devices, per_device(): lax.all_gather(image.astype(jnp.bfloat16), 'tensor', axis=1, tiled=True)  41.7 us
    psum x1, blocking collectives, per_device(): attn_sum, router_total = lax.psum((attn_terms, router_term), 'shard')  34.2 us
  transfers between devices with their start and end apart: 16, of which 15 were waited for; matrix products, arithmetic and copies ran while one was open for 4% of the time, Pallas kernels for 0%

profile of v1, /device:TPU:8, one launch (start us, length us, event | category | flops | bytes accessed | tf_op | source)
XLA Modules:
  0.0 1049.2 jit_solution(16675939102367596864)
XLA Ops:
  8.0 450.4 %while.26 = (s32[]{:T(128)}, bf16[8,256,576]{1,2,0:T(8,128)(2,1)S(1)}, bf16[8,256,288]{1,2,0:T(8,128)(2,1)S(1)}, bf16[8,256,72]{1,2,0:T(8,128)(2,1)}, s32[]{:T(128)}, /*index=5*/s32[]{:T(128)}, s32[]{:T(128)}) while((s32[]{:T(128)}, bf16[8,256,576]{1,2,0:T(8,128)(2,1)S(1)}, bf16[8,256,288]{1,2,0:T(8,128)(2,1)S(1)}, ...), condition=%wide.region_1.2_spmd, body=%wide.region_0.1_spmd.sunk | while | flops 2 | bytes 4608145 | solution.py:61
  9.5 56.6 %all-gather.27.cloned.1.call-done = bf16[1,256,2304]{1,2,0:T(8,128)(2,1)} async-done(((bf16[1,256,72]{1,2,0:T(8,128)(2,1)}), bf16[1,256,2304]{1,2,0:T(8,128)(2,1)}) %all-gather.27.cloned.1.call-update) | async-done | bytes 1179664 | tf_op jit(solution)/shard_map/while/body/eval_jaxpr/all_gather | solution.py:56
  69.5 52.5 %all-gather.27.cloned.1.call-done = bf16[1,256,2304]{1,2,0:T(8,128)(2,1)} async-done(((bf16[1,256,72]{1,2,0:T(8,128)(2,1)}), bf16[1,256,2304]{1,2,0:T(8,128)(2,1)}) %all-gather.27.cloned.1.call-update) | async-done | bytes 1179664 | tf_op jit(solution)/shard_map/while/body/eval_jaxpr/all_gather | solution.py:56
  125.4 52.5 %all-gather.27.cloned.1.call-done = bf16[1,256,2304]{1,2,0:T(8,128)(2,1)} async-done(((bf16[1,256,72]{1,2,0:T(8,128)(2,1)}), bf16[1,256,2304]{1,2,0:T(8,128)(2,1)}) %all-gather.27.cloned.1.call-update) | async-done | bytes 1179664 | tf_op jit(solution)/shard_map/while/body/eval_jaxpr/all_gather | solution.py:56
  181.3 52.2 %all-gather.27.cloned.1.call-done = bf16[1,256,2304]{1,2,0:T(8,128)(2,1)} async-done(((bf16[1,256,72]{1,2,0:T(8,128)(2,1)}), bf16[1,256,2304]{1,2,0:T(8,128)(2,1)}) %all-gather.27.cloned.1.call-update) | async-done | bytes 1179664 | tf_op jit(solution)/shard_map/while/body/eval_jaxpr/all_gather | solution.py:56
  236.9 52.2 %all-gather.27.cloned.1.call-done = bf16[1,256,2304]{1,2,0:T(8,128)(2,1)} async-done(((bf16[1,256,72]{1,2,0:T(8,128)(2,1)}), bf16[1,256,2304]{1,2,0:T(8,128)(2,1)}) %all-gather.27.cloned.1.call-update) | async-done | bytes 1179664 | tf_op jit(solution)/shard_map/while/body/eval_jaxpr/all_gather | solution.py:56
  292.5 52.2 %all-gather.27.cloned.1.call-done = bf16[1,256,2304]{1,2,0:T(8,128)(2,1)} async-done(((bf16[1,256,72]{1,2,0:T(8,128)(2,1)}), bf16[1,256,2304]{1,2,0:T(8,128)(2,1)}) %all-gather.27.cloned.1.call-update) | async-done | bytes 1179664 | tf_op jit(solution)/shard_map/while/body/eval_jaxpr/all_gather | solution.py:56
  348.1 52.5 %all-gather.27.cloned.1.call-done = bf16[1,256,2304]{1,2,0:T(8,128)(2,1)} async-done(((bf16[1,256,72]{1,2,0:T(8,128)(2,1)}), bf16[1,256,2304]{1,2,0:T(8,128)(2,1)}) %all-gather.27.cloned.1.call-update) | async-done | bytes 1179664 | tf_op jit(solution)/shard_map/while/body/eval_jaxpr/all_gather | solution.py:56
  404.0 52.5 %all-gather.27.cloned.1.call-done = bf16[1,256,2304]{1,2,0:T(8,128)(2,1)} async-done(((bf16[1,256,72]{1,2,0:T(8,128)(2,1)}), bf16[1,256,2304]{1,2,0:T(8,128)(2,1)}) %all-gather.27.cloned.1.call-update) | async-done | bytes 1179664 | tf_op jit(solution)/shard_map/while/body/eval_jaxpr/all_gather | solution.py:56
  458.5 3.6 fusion.83
  462.3 70.5 %reduce-scatter.2.cloned.1.call-done = f32[1,576,288]{1,2,0:T(8,128)} async-done(((f32[8,576,288]{1,2,0:T(8,128)}), f32[1,576,288]{1,2,0:T(8,128)}) %reduce-scatter.2.cloned.1.call-update) | async-done | bytes 663568 | tf_op jit(solution)/shard_map/reduce_scatter | solution.py:65
  532.8 2.1 fusion.48
  534.9 12.2 %psum.63 = f32[1]{0:T(128)} all-reduce(f32[1]{0:T(128)} %bitcast.4), channel_id=1, replica_groups=mesh['shard'=8,'tensor'=4,'section'=8] {'section'}, use_global_device_ids=true, to_apply=%region_4.5 | all-reduce | flops 1 | bytes 8 | tf_op jit(solution)/shard_map/psum | solution.py:71
  547.1 12.5 %psum.64 = f32[1]{0:T(128)} all-reduce(f32[1]{0:T(128)} %psum.63), channel_id=1, replica_groups=mesh['shard'=8,'tensor'=4,'section'=8] {'tensor'}, use_global_device_ids=true, to_apply=%region_5.6 | all-reduce | flops 1 | bytes 8 | tf_op jit(solution)/shard_map/psum | solution.py:71
  560.4 1.9 copy.32
  563.0 62.8 %all-gather.19.cloned.1.call-done = bf16[1,2304,288]{2,0,1:T(2,128)(2,1)} async-done(((bf16[1,576,288]{2,0,1:T(2,128)(2,1)}), bf16[1,2304,288]{2,0,1:T(2,128)(2,1)}) %all-gather.19.cloned.1.call-update) | async-done | bytes 1327120 | tf_op jit(solution)/shard_map/all_gather | solution.py:78
  625.9 8.4 copy.33
  634.3 29.2 %all-gather.17.cloned.1.call-done = bf16[1,576,2304]{1,2,0:T(8,128)(2,1)} async-done(((bf16[1,576,288]{1,2,0:T(8,128)(2,1)}), bf16[1,576,2304]{1,2,0:T(8,128)(2,1)}) %all-gather.17.cloned.1.call-update) | async-done | bytes 2654224 | tf_op jit(solution)/shard_map/all_gather | solution.py:79
  663.5 3.8 fusion.29
  668.1 41.7 %all-gather.25.cloned.1.call-done = bf16[4,576,288]{1,2,0:T(8,128)(2,1)} async-done(((bf16[1,576,288]{1,2,0:T(8,128)(2,1)}), bf16[4,576,288]{1,2,0:T(8,128)(2,1)}) %all-gather.25.cloned.1.call-update) | async-done | bytes 1327120 | tf_op jit(solution)/shard_map/all_gather | solution.py:80
  709.9 2.1 copy.34
  712.0 2.0 reshape.184
  714.0 24.7 %all-gather.15.cloned.1.call-done = bf16[1,576,2304]{1,2,0:T(8,128)(2,1)} async-done(((bf16[1,576,288]{1,2,0:T(8,128)(2,1)}), bf16[1,576,2304]{1,2,0:T(8,128)(2,1)}) %all-gather.15.cloned.1.call-update) | async-done | bytes 2654224 | tf_op jit(solution)/shard_map/all_gather | solution.py:81
  738.8 4.2 fusion.21
  743.2 19.7 %psum.68 = f32[8,8]{1,0:T(8,128)S(1)} all-reduce(f32[8,8]{1,0:T(8,128)S(1)} %fusion.84), channel_id=1, replica_groups=mesh['shard'=8,'tensor'=4,'section'=8] {'shard'}, use_global_device_ids=true, to_apply=%region_9.10 | all-reduce | flops 64 | bytes 512 | tf_op jit(solution)/shard_map/psum | solution.py:102
  764.9 15.1 %all-gather.4 = s32[8,1,256]{2,1,0:T(1,128)S(1)} all-gather(s32[1,1,256]{2,1,0:T(1,128)S(1)} %bitcast.152), channel_id=1, replica_groups=mesh['shard'=8,'tensor'=4,'section'=8] {'shard'}, dimensions={0}, use_global_device_ids=true | all-gather | bytes 9216 | tf_op jit(solution)/shard_map/all_gather | solution.py:124
  780.4 10.0 all-gather.21.cloned.1.call-done
  790.4 2.0 fusion.44
  792.3 2.0 fusion.43
  794.3 2.0 fusion.42
  796.3 2.0 fusion.41
  798.3 2.0 fusion.40
  800.3 56.8 %all-reduce.6 = bf16[5,256,288]{1,2,0:T(8,128)(2,1)S(1)} all-reduce(f32[5,256,288]{1,2,0:T(8,128)} %fusion.40), channel_id=1, replica_groups=mesh['shard'=8,'tensor'=4,'section'=8] {'tensor'}, use_global_device_ids=true, to_apply=%region_7.8 | all-reduce | flops 368640 | bytes 2211840 | tf_op jit(solution)/shard_map/psum | solution.py:97
  857.9 1.4 convolution_bitcast_fusion.2
  859.3 1.4 convolution_bitcast_fusion.1
  860.7 1.4 convolution_bitcast_fusion
  862.3 48.2 %all-reduce.7 = bf16[3,256,576]{1,2,0:T(8,128)(2,1)S(1)} all-reduce(f32[3,256,576]{1,2,0:T(8,128)S(1)} %pad_maximum_fusion), channel_id=1, replica_groups=mesh['shard'=8,'tensor'=4,'section'=8] {'section'}, use_global_device_ids=true, to_apply=%region_6.7 | all-reduce | flops 442368 | bytes 2654208 | tf_op jit(solution)/shard_map/psum | solution.py:90
  910.8 34.2 %all-reduce = (f32[8,576]{1,0:T(8,128)S(1)}, f32[2,72]{1,0:T(2,128)S(1)}, f32[2,72]{1,0:T(2,128)S(1)}) all-reduce(f32[8,576]{1,0:T(8,128)S(1)} %fusion.45, f32[2,72]{1,0:T(2,128)S(1)} %get-tuple-element.173, f32[2,72]{1,0:T(2,128)S(1)} %get-tuple-element.172), channel_id=1, replica_groups=mesh['shard'=8,'tensor'=4,'section'=8] {'shard'}, use_global_device_ids=true, to_apply=%region_11.12 | all-reduce | flops 4896 | bytes 39168 | tf_op jit(solution)/shard_map/psum | solution.py:131
  945.6 2.3 fusion.34
  949.1 2.5 copy.35
  951.6 18.0 %while.27 = (s32[]{:T(128)}, f32[4,512,288]{1,2,0:T(8,128)S(1)}, f32[4,512]{1,0:T(4,128)S(1)}, s32[4]{0:T(128)S(1)}, s32[]{:T(128)}, /*index=5*/s32[2048]{0:T(10...) while((s32[]{:T(128)}, f32[4,512,288]{1,2,0:T(8,128)S(1)}, f32[4,512]{1,0:T(4,128)S(1)}, ...), condition=%wide.region_18.19_spmd, body=%wide.region_16.18_spmd.sunk | while | flops 609222656 | bytes 1798293 | solution.py:145
  953.0 2.5 fusion.99
  957.4 2.5 fusion.99
  961.9 2.5 fusion.99
  966.5 2.5 fusion.99
  970.6 1.7 broadcast_divide_fusion
  972.3 65.8 %all-reduce.5.cloned.1.call-done = f32[4,576,288]{1,2,0:T(8,128)} async-done(((f32[4,576,288]{1,2,0:T(8,128)}), f32[4,576,288]{1,2,0:T(8,128)}) %all-reduce.5.cloned.1.call-update) | async-done | bytes 2654224 | tf_op jit(solution)/shard_map/psum | solution.py:131
  1038.1 3.7 broadcast_multiply_fusion
  (128 shorter events, 39.5 us)
Async XLA Ops:
  8.0 735.1 %copy-start = (bf16[8,256]{1,0:T(8,128)(2,1)S(1)}, bf16[8,256]{1,0:T(8,128)(2,1)}, u32[]{:S(2)}) copy-start(bf16[8,256]{1,0:T(8,128)(2,1)} %param.13) | copy-start | bytes 12292
  8.1 58.1 %all-gather.27.cloned.1.call-start = ((), (), s32[]{:S(2)}) async-start(), calls=%async_computation.9 | async-start | bytes 1216512 | tf_op jit(solution)/shard_map/while/body/eval_jaxpr/all_gather | solution.py:56
  68.0 54.0 %all-gather.27.cloned.1.call-start = ((), (), s32[]{:S(2)}) async-start(), calls=%async_computation.9 | async-start | bytes 1216512 | tf_op jit(solution)/shard_map/while/body/eval_jaxpr/all_gather | solution.py:56
  124.0 54.0 %all-gather.27.cloned.1.call-start = ((), (), s32[]{:S(2)}) async-start(), calls=%async_computation.9 | async-start | bytes 1216512 | tf_op jit(solution)/shard_map/while/body/eval_jaxpr/all_gather | solution.py:56
  179.9 53.7 %all-gather.27.cloned.1.call-start = ((), (), s32[]{:S(2)}) async-start(), calls=%async_computation.9 | async-start | bytes 1216512 | tf_op jit(solution)/shard_map/while/body/eval_jaxpr/all_gather | solution.py:56
  235.4 53.7 %all-gather.27.cloned.1.call-start = ((), (), s32[]{:S(2)}) async-start(), calls=%async_computation.9 | async-start | bytes 1216512 | tf_op jit(solution)/shard_map/while/body/eval_jaxpr/all_gather | solution.py:56
  291.0 53.7 %all-gather.27.cloned.1.call-start = ((), (), s32[]{:S(2)}) async-start(), calls=%async_computation.9 | async-start | bytes 1216512 | tf_op jit(solution)/shard_map/while/body/eval_jaxpr/all_gather | solution.py:56
  346.6 54.0 %all-gather.27.cloned.1.call-start = ((), (), s32[]{:S(2)}) async-start(), calls=%async_computation.9 | async-start | bytes 1216512 | tf_op jit(solution)/shard_map/while/body/eval_jaxpr/all_gather | solution.py:56
  402.5 54.0 %all-gather.27.cloned.1.call-start = ((), (), s32[]{:S(2)}) async-start(), calls=%async_computation.9 | async-start | bytes 1216512 | tf_op jit(solution)/shard_map/while/body/eval_jaxpr/all_gather | solution.py:56
  458.4 3.7 copy-start.5
  458.5 3.7 copy-start.7
  458.5 74.3 %reduce-scatter.2.cloned.1.call-start = ((), (), s32[]{:S(2)}) async-start(), calls=%async_computation.1 | async-start | bytes 6635520 | tf_op jit(solution)/shard_map/reduce_scatter | solution.py:65
  462.2 70.6 %copy-start.8 = (f32[1,576,288]{1,2,0:T(8,128)S(1)}, f32[1,576,288]{1,2,0:T(8,128)}, u32[]{:S(2)}) copy-start(f32[1,576,288]{1,2,0:T(8,128)} %param.16) | copy-start | bytes 1990660
  462.2 163.7 %all-gather.19.cloned.1.call-start = ((), (), s32[]{:S(2)}) async-start(), calls=%async_computation.4 | async-start | bytes 4423680 | tf_op jit(solution)/shard_map/all_gather | solution.py:78
  534.9 27.6 %copy-start.1 = (bf16[1,576,288]{1,2,0:T(8,128)(2,1)}, bf16[1,576,288]{1,2,0:T(8,128)(2,1)S(1)}, u32[]{:S(2)}) copy-start(bf16[1,576,288]{1,2,0:T(8,128)(2,1)S(1)} %get-tuple-element.206) | copy-start | bytes 995332
  560.4 73.9 %copy-start.3 = (bf16[1,576,288]{1,2,0:T(8,128)(2,1)}, bf16[1,576,288]{1,2,0:T(8,128)(2,1)S(1)}, u32[]{:S(2)}) copy-start(bf16[1,576,288]{1,2,0:T(8,128)(2,1)S(1)} %fusion.50) | copy-start | bytes 995332
  562.4 101.1 %all-gather.17.cloned.1.call-start = ((), (), s32[]{:S(2)}) async-start(), calls=%async_computation.3 | async-start | bytes 3317760 | tf_op jit(solution)/shard_map/all_gather | solution.py:79
  563.0 146.9 %all-gather.25.cloned.1.call-start = ((), (), s32[]{:S(2)}) async-start(), calls=%async_computation.8 | async-start | bytes 1843200 | tf_op jit(solution)/shard_map/all_gather | solution.py:80
  667.3 71.4 %all-gather.15.cloned.1.call-start = ((), (), s32[]{:S(2)}) async-start(), calls=%async_computation.2 | async-start | bytes 3317760 | tf_op jit(solution)/shard_map/all_gather | solution.py:81
  668.1 70.7 %copy-start.2 = (bf16[1,576,288]{1,2,0:T(8,128)(2,1)S(1)}, bf16[1,576,288]{1,2,0:T(8,128)(2,1)}, u32[]{:S(2)}) copy-start(bf16[1,576,288]{1,2,0:T(8,128)(2,1)} %copy-done.1) | copy-start | bytes 995332
  668.1 122.3 %all-gather.21.cloned.1.call-start = ((), (), s32[]{:S(2)}) async-start(), calls=%async_computation.5 | async-start | bytes 3317760 | tf_op jit(solution)/shard_map/all_gather | solution.py:83
  714.0 48.9 %copy-start.11 = (f32[8,8]{1,0:T(8,128)S(1)}, f32[8,8]{1,0:T(8,128)}, u32[]{:S(2)}) copy-start(f32[8,8]{1,0:T(8,128)} %param.17) | copy-start | bytes 772
  714.0 50.8 %copy-start.12 = (s32[256]{0:T(256)S(1)}, s32[256]{0:T(256)}, u32[]{:S(2)}) copy-start(s32[256]{0:T(256)} %param.14) | copy-start | bytes 3076
  714.0 66.0 %copy-start.9 = (bf16[2,256,72]{1,2,0:T(8,128)(2,1)S(1)}, bf16[2,256,72]{1,2,0:T(8,128)(2,1)}, u32[]{:S(2)}) copy-start(bf16[2,256,72]{1,2,0:T(8,128)(2,1)} %param.15) | copy-start | bytes 221188
  714.0 76.3 %copy-start.6 = (bf16[8,256,576]{1,2,0:T(8,128)(2,1)S(1)}, bf16[8,256,576]{1,2,0:T(8,128)(2,1)}, u32[]{:S(2)}) copy-start(bf16[8,256,576]{1,2,0:T(8,128)(2,1)} %copy-done.5) | copy-start | bytes 7077892
  743.0 206.1 %all-gather.23.cloned.1.call-start = ((), (), s32[]{:S(2)}) async-start(), calls=%async_computation.7 | async-start | bytes 1327104 | tf_op jit(solution)/shard_map/all_gather | solution.py:125
  857.8 180.3 %all-reduce.5.cloned.1.call-start = ((), (), s32[]{:S(2)}) async-start(), calls=%async_computation.6 | async-start | bytes 5898240 | tf_op jit(solution)/shard_map/psum | solution.py:131
  947.8 0.7 copy-start.13
  947.8 3.8 copy-start.4
  969.9 0.7 copy-start.10
Sparse Core Ops, SparseCore 0:
  12.1 53.9 all-gather.26
  72.1 49.8 all-gather.26
  128.0 49.8 all-gather.26
  183.6 49.8 all-gather.26
  239.2 49.8 all-gather.26
  294.8 49.8 all-gather.26
  350.7 49.8 all-gather.26
  406.6 49.8 all-gather.26
Sparse Core Ops, SparseCore 1:
  462.3 70.4 reduce-scatter.1
  562.5 63.3 all-gather.18
  627.7 35.8 all-gather.16
  667.4 42.4 all-gather.24
  711.9 26.8 all-gather.14
  743.1 47.2 all-gather.20
  857.9 39.4 all-gather.22
  947.9 90.1 all-reduce.4
